TPU v7x, 512 devices: a whole 4x4x16 slice. The times are simulated.
512 devices in a mesh: req: 64 (over y, z), head: 8 (over x, core).
Axes of the slice: x: 4, y: 4, z: 16, core: 2. Of those that a mesh axis runs over, the one named last changes fastest.
Arguments:
- tokens: bfloat16 [256, 2048], P('req'), may hold values from -1.1953125 to 1.1953125
- lengths: int32 [256], replicated, may hold values from 1 to 1021, as said below
- kv_cache: bfloat16 [1, 2, 65536, 8, 128], P(None, None, 'req', 'head'), may hold values from -24 to 24
- w_qkv: bfloat16 [1, 2048, 8, 512], P(None, 'req', 'head'), may hold values from -0.125 to 0.125
- w_headgate: bfloat16 [1, 2048, 16], P(None, None, 'head'), may hold values from -0.125 to 0.125
- w_out: bfloat16 [1, 2048, 2048], P(None, 'head', 'req'), may hold values from -0.5 to 0.5
- in_gain: float32 [1, 2048], replicated, may hold values from 0.5 to 1.5
- q_gain: float32 [1, 128], replicated, may hold values from 0.1 to 1.9
- k_gain: float32 [1, 128], replicated, may hold values from 0.1 to 1.9
- post_gain: float32 [1, 2048], replicated, may hold values from 0.5 to 1.5
- w_gate: bfloat16 [1, 2048, 6144], P(None, 'head', 'req'), may hold values from -0.125 to 0.125
- w_up: bfloat16 [1, 2048, 6144], P(None, 'head', 'req'), may hold values from -0.125 to 0.125
- w_down: bfloat16 [1, 6144, 2048], P(None, 'req', 'head'), may hold values from -0.078125 to 0.078125
- final_gain: float32 [2048], replicated, may hold values from 0.5 to 1.5
- w_vocab: bfloat16 [2048, 131072], P(None, ('req', 'head')), may hold values from -0.125 to 0.125
Outputs:
- logits: bfloat16 [256, 131072], P(None, ('req', 'head'))
Inputs may be any that keep to these rules, and one draw needn't show every extreme that they name: On every index of req the lengths of its 4 requests sum to at most 1024. On 8 indices, drawn anew, they sum to exactly 1024 and one request there is longer than 512; on one of these the other requests hold one token each. On every other index each length is at most 128 and one is exactly 128.
All inputs are finite; a program needn't handle non-finite values.
Results may differ from a plain program's by a relative error of at most 0.015.
Values may be sent and summed in bfloat16 or wider, within the bound.
No kernel may reach another device: no remote copies, remote signals or barrier semaphores. Data moves between devices by JAX's collectives and lax.ppermute only.
A program may use at most 64 MiB of HBM per device.

v0:
```python
import jax
import jax.numpy as jnp
from jax import lax
from jax.sharding import Mesh
from jax.sharding import PartitionSpec as P

EPSILON = 1e-06
ROPE_THETA = 1000000.0
Y, Z, X, C = (4, 16, 4, 2)
F32, BF16 = (jnp.float32, jnp.bfloat16)


def rms_scale(values, gain):
    mean_square = jnp.mean(values * values, axis=-1, keepdims=True)
    return values * lax.rsqrt(mean_square + EPSILON) * gain


def rotate(values, cosine, sine):
    half = values.shape[-1] // 2
    a, b = (values[..., :half], values[..., half:])
    return jnp.concatenate([a * cosine - b * sine, b * cosine + a * sine], axis=-1)


def swap(values, axes):
    return lax.all_to_all(values, axes, split_axis=0, concat_axis=0, tiled=True)


def spread(values, axes, count):
    return swap(jnp.broadcast_to(values[None], (count,) + values.shape), axes)


def local(
    tokens,
    lengths,
    kv_cache,
    w_qkv,
    w_headgate,
    w_out,
    in_gain,
    q_gain,
    k_gain,
    post_gain,
    w_gate,
    w_up,
    w_down,
    final_gain,
    w_vocab,
):
    rows, width = tokens.shape
    head_dim = q_gain.shape[1]
    columns = w_qkv.shape[3]
    req = lax.axis_index(("y", "z"))
    ix, ic = (lax.axis_index("x"), lax.axis_index("c"))
    qkv_block = lax.all_gather(w_qkv[0, :, 0], "y", axis=0, tiled=True)
    out_part = lax.all_gather(w_out[0].T, "z", axis=0, tiled=True)
    out_block = lax.all_gather(out_part, "y", axis=0, tiled=True)
    gate_up = jnp.concatenate([w_gate[0].T, w_up[0].T], axis=0)
    gate_up = lax.all_gather(gate_up, "x", axis=0)
    down = lax.all_gather(w_down[0], "x", axis=0)
    positions = lax.dynamic_slice_in_dim(lengths, req * rows, rows)
    starts = jnp.cumsum(positions) - positions
    limits = starts + positions
    normed = rms_scale(tokens.astype(F32), in_gain[0]).astype(BF16)
    head_gate = jax.nn.sigmoid(jnp.dot(normed, w_headgate[0], preferred_element_type=F32))
    depth = width // (Y * Z)
    sent = normed.reshape(rows, Y, Z, depth).transpose(2, 0, 1, 3).reshape(Z, rows, Y * depth)
    arrived = swap(sent, "z").reshape(Z * rows, Y * depth)
    part = jnp.dot(arrived, qkv_block, preferred_element_type=F32).astype(BF16)
    qkv = jnp.sum(swap(part.reshape(Z, rows, columns), "z").astype(F32), axis=0)
    half = head_dim // 2
    frequency = ROPE_THETA ** (-2.0 * jnp.arange(half, dtype=F32) / head_dim)
    angles = positions.astype(F32)[:, None] * frequency[None, :]
    cosine, sine = (jnp.cos(angles), jnp.sin(angles))
    query = qkv[:, : 2 * head_dim].reshape(rows, 2, head_dim)
    query = rotate(rms_scale(query, q_gain[0]), cosine[:, None], sine[:, None]).astype(BF16)
    key = qkv[:, 2 * head_dim : 3 * head_dim]
    key = rotate(rms_scale(key, k_gain[0]), cosine, sine).astype(BF16)
    value = qkv[:, 3 * head_dim :].astype(BF16)
    scale = head_dim ** (-0.5)
    keys, values = (kv_cache[0, 0, :, 0], kv_cache[0, 1, :, 0])
    slots = keys.shape[0]
    score = jnp.einsum("rqd,sd->rqs", query, keys, preferred_element_type=F32) * scale
    slot = jnp.arange(slots, dtype=jnp.int32)
    inside = (slot[None, :] >= starts[:, None]) & (slot[None, :] < limits[:, None])
    weight = jnp.where(inside[:, None, :], jnp.exp(score), 0.0)
    own = jnp.exp(jnp.sum(query.astype(F32) * key.astype(F32)[:, None], axis=-1) * scale)
    total = jnp.sum(weight, axis=-1) + own
    summed = jnp.einsum("rqs,sd->rqd", weight.astype(BF16), values, preferred_element_type=F32)
    summed = summed + own.astype(BF16).astype(F32)[..., None] * value.astype(F32)[:, None]
    attended = summed / total[..., None]
    mixed = (attended * head_gate[..., None]).astype(BF16).reshape(rows, 2 * head_dim)
    part = lax.dot_general(mixed, out_block, (((1,), (1,)), ((), ())), preferred_element_type=F32)
    projected = jnp.sum(spread(part, ("x", "c"), X * C), axis=0)
    stream = (tokens.astype(F32) + projected).astype(BF16)
    normed_two = rms_scale(stream.astype(F32), post_gain[0]).astype(BF16)

    def mine(array):
        row = lax.dynamic_slice_in_dim(array, ix, 1, 0).reshape(X, C, width // (X * C))
        return lax.dynamic_slice_in_dim(row, ic, 1, 1).reshape(1, width // C)

    batch = spread(mine(normed_two), ("y", "z"), Y * Z).reshape(Y * Z, width // C)
    gate_up = gate_up.transpose(1, 0, 2).reshape(gate_up.shape[1], width // C)
    part = lax.dot_general(batch, gate_up, (((1,), (1,)), ((), ())), preferred_element_type=F32)
    both = jnp.sum(lax.all_gather(part, "c", axis=0), axis=0)
    units = w_gate.shape[2]
    hidden = (jax.nn.silu(both[:, :units]) * both[:, units:]).astype(BF16)
    down = down.transpose(1, 0, 2).reshape(units, width // C)
    part = jnp.dot(hidden, down, preferred_element_type=F32).astype(BF16)
    lowered = jnp.sum(swap(part.reshape(Y * Z, 1, width // C), ("y", "z")).astype(F32), axis=0)
    piece = (mine(stream).astype(F32) + lowered).astype(BF16)
    piece = spread(piece, ("y", "z"), Y * Z).reshape(Y * Z, width // C)
    piece = spread(piece, "x", X).reshape(X * Y * Z, width // C)
    whole = lax.all_gather(piece, "c", axis=0)
    mean_square = jnp.sum(jnp.square(whole.astype(F32)), axis=(0, 2)) / width
    gain = final_gain.reshape(X, C, width // (X * C)).transpose(1, 0, 2).reshape(C, 1, width // C)
    final = (whole.astype(F32) * lax.rsqrt(mean_square + EPSILON)[None, :, None] * gain).astype(
        BF16
    )
    vocab = w_vocab.reshape(X, C, width // (X * C), w_vocab.shape[1]).transpose(1, 0, 2, 3)
    vocab = vocab.reshape(C, width // C, w_vocab.shape[1])
    logits = jnp.dot(final[0], vocab[0], preferred_element_type=F32)
    logits = logits + jnp.dot(final[1], vocab[1], preferred_element_type=F32)
    logits = logits.astype(BF16).reshape(X, Y * Z, w_vocab.shape[1]).transpose(1, 0, 2)
    return logits.reshape(X * Y * Z, w_vocab.shape[1])


def solution(mesh):
    fine = Mesh(mesh.devices.reshape(Y, Z, X, C), ("y", "z", "x", "c"))
    req, head = (("y", "z"), ("x", "c"))
    in_specs = (
        P(req, None),
        P(),
        P(None, None, req, head, None),
        P(None, req, head, None),
        P(None, None, head),
        P(None, head, req),
        P(),
        P(),
        P(),
        P(),
        P(None, head, req),
        P(None, head, req),
        P(None, req, head),
        P(),
        P(None, req + head),
    )
    out_specs = P(None, req + head)
    return jax.shard_map(local, mesh=fine, in_specs=in_specs, out_specs=out_specs, check_vma=False)
```

profile of v0, /device:TPU:1, one launch (start us, length us, event | category | flops | bytes accessed | tf_op | source)
XLA Modules:
  0.0 240.8 jit_solution(1843471291022749129)
XLA Ops:
  6.5 0.9 fusion.26
  7.5 0.8 fusion.28
  9.1 15.7 %all-to-all-start = ((bf16[16,4,128]{2,1,0:T(4,128)(2,1)}), bf16[16,4,128]{2,1,0:T(4,128)(2,1)S(1)}, u32[]{:S(2)}, u32[]{:S(2)}) async-start(bf16[16,4,128]{2,1,0:T(4,128)(2,1)} %copy.39), calls=%async_computation | async-start | bytes 32768 | tf_op jit(solution)/shard_map/all_to_all | solution.py:25
  24.9 27.0 %all_gather.28 = bf16[512,256]{1,0:T(8,128)(2,1)} all-gather(bf16[32,256]{1,0:T(8,128)(2,1)} %bitcast.114), channel_id=1, replica_groups=mesh['y'=4,'z'=16,'x'=4,'c'=2] {'z'}, dimensions={0}, use_global_device_ids=true | all-gather | bytes 278528 | tf_op jit(solution)/shard_map/all_gather | solution.py:55
  52.0 0.8 dynamic-slice_bitcast_fusion
  53.8 10.2 %all-gather = bf16[1,128,1,512]{3,1,2,0:T(8,128)(2,1)S(1)} all-gather(bf16[1,32,1,512]{3,1,2,0:T(8,128)(2,1)} %param.18), channel_id=2, replica_groups=mesh['y'=4,'z'=16,'x'=4,'c'=2] {'y'}, dimensions={1}, use_global_device_ids=true | all-gather | bytes 163840 | tf_op jit(solution)/shard_map/all_gather | solution.py:54
  64.8 7.5 %all-to-all-start.1 = ((bf16[16,4,512]{2,1,0:T(4,128)(2,1)}), bf16[16,4,512]{2,1,0:T(4,128)(2,1)S(1)}, u32[]{:S(2)}, u32[]{:S(2)}) async-start(bf16[16,4,512]{2,1,0:T(4,128)(2,1)} %reshape.262), calls=%async_computation.1 | async-start | bytes 131072 | tf_op jit(solution)/shard_map/all_to_all | solution.py:25
  72.5 11.4 %all-to-all-done.1 = bf16[16,4,512]{2,1,0:T(4,128)(2,1)S(1)} async-done(((bf16[16,4,512]{2,1,0:T(4,128)(2,1)}), bf16[16,4,512]{2,1,0:T(4,128)(2,1)S(1)}, u32[]{:S(2)}, u32[]{:S(2)}) %all-to-all-start.1) | async-done | bytes 65568 | tf_op jit(solution)/shard_map/all_to_all | solution.py:25
  85.1 2.8 %all-gather.6.cloned.1.call-done = bf16[2048,256]{1,0:T(8,128)(2,1)} async-done(((bf16[512,256]{1,0:T(8,128)(2,1)}), bf16[2048,256]{1,0:T(8,128)(2,1)}) %all-gather.6.cloned.1.call-update) | async-done | bytes 1048592 | tf_op jit(solution)/shard_map/all_gather | solution.py:56
  87.9 1.7 fusion.14
  90.4 14.3 %all-to-all-start.2 = ((f32[8,4,2048]{2,1,0:T(4,128)}), f32[8,4,2048]{2,1,0:T(4,128)S(1)}, u32[]{:S(2)}, u32[]{:S(2)}) async-start(f32[8,4,2048]{2,1,0:T(4,128)} %broadcast_in_dim.26), calls=%async_computation.2 | async-start | bytes 524288 | tf_op jit(solution)/shard_map/all_to_all | solution.py:25
  104.6 6.5 %all-to-all-done.2 = f32[8,4,2048]{2,1,0:T(4,128)S(1)} async-done(((f32[8,4,2048]{2,1,0:T(4,128)}), f32[8,4,2048]{2,1,0:T(4,128)S(1)}, u32[]{:S(2)}, u32[]{:S(2)}) %all-to-all-start.2) | async-done | bytes 262176 | tf_op jit(solution)/shard_map/all_to_all | solution.py:25
  113.4 1.4 reduce.7
  115.6 6.1 %all-to-all-start.3 = ((bf16[64,2,512]{2,1,0:T(2,128)(2,1)}), bf16[64,2,512]{2,1,0:T(2,128)(2,1)S(1)}, u32[]{:S(2)}, u32[]{:S(2)}) async-start(bf16[64,2,512]{2,1,0:T(2,128)(2,1)} %reshape.284), calls=%async_computation.3 | async-start | bytes 262144 | tf_op jit(solution)/shard_map/all_to_all | solution.py:25
  121.7 9.8 %all_gather.34 = bf16[4,96,256]{2,1,0:T(8,128)(2,1)S(1)} all-gather(bf16[1,96,256]{2,1,0:T(8,128)(2,1)S(1)} %copy-done.6), channel_id=1, replica_groups=mesh['y'=4,'z'=16,'x'=4,'c'=2] {'x'}, dimensions={0}, use_global_device_ids=true | all-gather | bytes 245760 | tf_op jit(solution)/shard_map/all_gather | solution.py:59
  131.6 9.9 %all-gather.1 = bf16[768,256]{1,0:T(8,128)(2,1)S(1)} all-gather(bf16[192,256]{1,0:T(8,128)(2,1)S(1)} %pad_maximum_fusion), channel_id=3, replica_groups=mesh['y'=4,'z'=16,'x'=4,'c'=2] {'x'}, dimensions={0}, use_global_device_ids=true | all-gather | bytes 491520 | tf_op jit(solution)/shard_map/all_gather | solution.py:58
  142.3 7.9 %all-gather.2 = f32[128,192]{1,0:T(8,128)S(1)} all-gather(f32[64,192]{1,0:T(8,128)S(1)} %fusion.22), channel_id=4, replica_groups=mesh['y'=4,'z'=16,'x'=4,'c'=2] {'c'}, dimensions={0}, use_global_device_ids=true | all-gather | bytes 147456 | tf_op jit(solution)/shard_map/all_gather | solution.py:104
  151.9 15.1 %all-to-all-start.4 = ((bf16[64,2,512]{2,1,0:T(2,128)(2,1)}), bf16[64,2,512]{2,1,0:T(2,128)(2,1)S(1)}, u32[]{:S(2)}, u32[]{:S(2)}) async-start(bf16[64,2,512]{2,1,0:T(2,128)(2,1)} %reshape.286), calls=%async_computation.4 | async-start | bytes 262144 | tf_op jit(solution)/shard_map/all_to_all | solution.py:25
  167.1 14.4 %all-to-all-done.4 = bf16[64,2,512]{2,1,0:T(2,128)(2,1)S(1)} async-done(((bf16[64,2,512]{2,1,0:T(2,128)(2,1)}), bf16[64,2,512]{2,1,0:T(2,128)(2,1)S(1)}, u32[]{:S(2)}, u32[]{:S(2)}) %all-to-all-start.4) | async-done | bytes 131104 | tf_op jit(solution)/shard_map/all_to_all | solution.py:25
  182.0 1.4 reduce.9
  183.5 21.1 %all_to_all.35 = bf16[64,2,512]{2,1,0:T(2,128)(2,1)S(1)} all-to-all(bf16[64,2,512]{2,1,0:T(2,128)(2,1)S(1)} %reshape.288), channel_id=1, replica_groups=mesh['y'=4,'z'=16,'x'=4,'c'=2] {'y','z'}, dimensions={0} | all-to-all | bytes 262144 | tf_op jit(solution)/shard_map/all_to_all | solution.py:25
  204.9 10.1 %all_to_all.36 = bf16[4,64,1024]{2,1,0:T(8,128)(2,1)} all-to-all(bf16[4,64,1024]{2,1,0:T(8,128)(2,1)S(1)} %broadcast_in_dim.31), channel_id=1, replica_groups=mesh['y'=4,'z'=16,'x'=4,'c'=2] {'x'}, dimensions={0} | all-to-all | bytes 1048576 | tf_op jit(solution)/shard_map/all_to_all | solution.py:25
  215.2 15.4 %all-gather.8.cloned.1.call-done = bf16[2,256,1024]{2,1,0:T(8,128)(2,1)} async-done(((bf16[1,256,1024]{2,1,0:T(8,128)(2,1)}), bf16[2,256,1024]{2,1,0:T(8,128)(2,1)}) %all-gather.8.cloned.1.call-update) | async-done | bytes 1048592 | tf_op jit(solution)/shard_map/all_gather | solution.py:113
  230.6 1.6 fusion
  (97 shorter events, 12.9 us)
Async XLA Ops:
  6.5 65.8 %copy-start = (bf16[1,2048,2]{1,2,0:T(2,128)(2,1)S(1)}, bf16[1,2048,2]{1,2,0:T(2,128)(2,1)}, u32[]{:S(2)}) copy-start(bf16[1,2048,2]{1,2,0:T(2,128)(2,1)} %param.19) | copy-start | bytes 24580
  6.5 77.6 %copy-start.9 = (f32[1,128]{1,0:T(1,128)S(1)}, f32[1,128]{1,0:T(1,128)}, u32[]{:S(2)}) copy-start(f32[1,128]{1,0:T(1,128)} %param.23) | copy-start | bytes 1540
  6.5 77.9 %copy-start.10 = (f32[1,128]{1,0:T(1,128)S(1)}, f32[1,128]{1,0:T(1,128)}, u32[]{:S(2)}) copy-start(f32[1,128]{1,0:T(1,128)} %param.22) | copy-start | bytes 1540
  6.5 78.2 %copy-start.11 = (bf16[1,2,1024,1,128]{4,2,3,1,0:T(8,128)(2,1)S(1)}, bf16[1,2,1024,1,128]{4,2,3,1,0:T(8,128)(2,1)}, u32[]{:S(2)}) copy-start(bf16[1,2,1024,1,128]{4,2,3,1,0:T(8,128)(2,1)} %param.17) | copy-start | bytes 1572868
  9.1 54.8 %all-to-all-start = ((bf16[16,4,128]{2,1,0:T(4,128)(2,1)}), bf16[16,4,128]{2,1,0:T(4,128)(2,1)S(1)}, u32[]{:S(2)}, u32[]{:S(2)}) async-start(bf16[16,4,128]{2,1,0:T(4,128)(2,1)} %copy.39), calls=%async_computation | async-start | bytes 32768 | tf_op jit(solution)/shard_map/all_to_all | solution.py:25
  24.9 63.0 %all-gather.6.cloned.1.call-start = ((), (), s32[]{:S(2)}) async-start(), calls=%async_computation.7 | async-start | bytes 1310720 | tf_op jit(solution)/shard_map/all_gather | solution.py:56
  64.8 19.1 %all-to-all-start.1 = ((bf16[16,4,512]{2,1,0:T(4,128)(2,1)}), bf16[16,4,512]{2,1,0:T(4,128)(2,1)S(1)}, u32[]{:S(2)}, u32[]{:S(2)}) async-start(bf16[16,4,512]{2,1,0:T(4,128)(2,1)} %reshape.262), calls=%async_computation.1 | async-start | bytes 131072 | tf_op jit(solution)/shard_map/all_to_all | solution.py:25
  87.9 23.3 %copy-start.3 = (bf16[4,2048]{1,0:T(4,128)(2,1)S(1)}, bf16[4,2048]{1,0:T(4,128)(2,1)}, u32[]{:S(2)}) copy-start(bf16[4,2048]{1,0:T(4,128)(2,1)} %param.15) | copy-start | bytes 49156
  87.9 24.0 %copy-start.8 = (f32[1,2048]{1,0:T(1,128)S(1)}, f32[1,2048]{1,0:T(1,128)}, u32[]{:S(2)}) copy-start(f32[1,2048]{1,0:T(1,128)} %param.24) | copy-start | bytes 24580
  90.4 31.4 %copy-start.6 = (bf16[1,96,256]{2,1,0:T(8,128)(2,1)S(1)}, bf16[1,96,256]{2,1,0:T(8,128)(2,1)}, u32[]{:S(2)}) copy-start(bf16[1,96,256]{2,1,0:T(8,128)(2,1)} %param.27) | copy-start | bytes 147460
  90.4 20.8 %all-to-all-start.2 = ((f32[8,4,2048]{2,1,0:T(4,128)}), f32[8,4,2048]{2,1,0:T(4,128)S(1)}, u32[]{:S(2)}, u32[]{:S(2)}) async-start(f32[8,4,2048]{2,1,0:T(4,128)} %broadcast_in_dim.26), calls=%async_computation.2 | async-start | bytes 524288 | tf_op jit(solution)/shard_map/all_to_all | solution.py:25
  111.2 20.4 %copy-start.4 = (bf16[1,256,96]{1,2,0:T(8,128)(2,1)S(1)}, bf16[1,256,96]{1,2,0:T(8,128)(2,1)}, u32[]{:S(2)}) copy-start(bf16[1,256,96]{1,2,0:T(8,128)(2,1)} %param.26) | copy-start | bytes 147460
  111.2 20.4 %copy-start.5 = (bf16[1,256,96]{1,2,0:T(8,128)(2,1)S(1)}, bf16[1,256,96]{1,2,0:T(8,128)(2,1)}, u32[]{:S(2)}) copy-start(bf16[1,256,96]{1,2,0:T(8,128)(2,1)} %param.25) | copy-start | bytes 147460
  115.6 26.3 %all-to-all-start.3 = ((bf16[64,2,512]{2,1,0:T(2,128)(2,1)}), bf16[64,2,512]{2,1,0:T(2,128)(2,1)S(1)}, u32[]{:S(2)}, u32[]{:S(2)}) async-start(bf16[64,2,512]{2,1,0:T(2,128)(2,1)} %reshape.284), calls=%async_computation.3 | async-start | bytes 262144 | tf_op jit(solution)/shard_map/all_to_all | solution.py:25
  151.9 29.6 %all-to-all-start.4 = ((bf16[64,2,512]{2,1,0:T(2,128)(2,1)}), bf16[64,2,512]{2,1,0:T(2,128)(2,1)S(1)}, u32[]{:S(2)}, u32[]{:S(2)}) async-start(bf16[64,2,512]{2,1,0:T(2,128)(2,1)} %reshape.286), calls=%async_computation.4 | async-start | bytes 262144 | tf_op jit(solution)/shard_map/all_to_all | solution.py:25
  167.1 63.6 %all-gather.8.cloned.1.call-start = ((), (), s32[]{:S(2)}) async-start(), calls=%async_computation.8 | async-start | bytes 1572864 | tf_op jit(solution)/shard_map/all_gather | solution.py:113
  204.8 10.3 %copy-start.7 = (f32[2048]{0:T(1024)S(1)}, f32[2048]{0:T(1024)}, u32[]{:S(2)}) copy-start(f32[2048]{0:T(1024)} %param.28) | copy-start | bytes 24580
  204.8 10.3 %copy-start.2 = (bf16[2048,256]{1,0:T(8,128)(2,1)S(1)}, bf16[2048,256]{1,0:T(8,128)(2,1)}, u32[]{:S(2)}) copy-start(bf16[2048,256]{1,0:T(8,128)(2,1)} %param.29) | copy-start | bytes 3145732
  230.6 1.6 copy-start.1
Sparse Core Ops, SparseCore 0:
  52.1 35.7 all-gather.5
  215.2 15.3 all-gather.7
where the time goes:
time: 242 us; the launch traced here: 241 us
  blocking collectives  96.2 us (40%)
  starting transfers between devices  58.9 us (24%)
  waiting for transfers between devices  50.5 us (21%)
  between operations  13.8 us (6%)
  other arithmetic  10.3 us (4%)
  local copies, waits for them, and re-layouts  7.77 us (3%)
  matrix products  3.4 us (1%)
    all_to_all x5, starting transfers between devices, swap(): return lax.all_to_all(values, axes, split_axis=0, concat_axis=0, tiled=True)  58.8 us
    all_to_all x5, waiting for transfers between devices, swap(): return lax.all_to_all(values, axes, split_axis=0, concat_axis=0, tiled=True)  32.3 us
    all_to_all x2, blocking collectives, swap(): return lax.all_to_all(values, axes, split_axis=0, concat_axis=0, tiled=True)  31.3 us
    all_gather x1, blocking collectives, local(): out_part = lax.all_gather(w_out[0].T, 'z', axis=0, tiled=True)  27 us
    all_gather x1, waiting for transfers between devices, local(): whole = lax.all_gather(piece, 'c', axis=0)  15.4 us
    all_gather x1, blocking collectives, local(): qkv_block = lax.all_gather(w_qkv[0, :, 0], 'y', axis=0, tiled=True)  10.2 us
    all_gather x1, blocking collectives, local(): gate_up = lax.all_gather(gate_up, 'x', axis=0)  9.93 us
    all_gather x1, blocking collectives, local(): down = lax.all_gather(w_down[0], 'x', axis=0)  9.83 us
  transfers between devices with their start and end apart: 7, of which 5 were waited for; matrix products, arithmetic and copies ran while one was open for 2% of the time, Pallas kernels for 0%

commit v1 on v0

--- a/solution.py
+++ b/solution.py
@@ -8,6 +8,13 @@
 ROPE_THETA = 1000000.0
 Y, Z, X, C = (4, 16, 4, 2)
 F32, BF16 = (jnp.float32, jnp.bfloat16)
+
+
+def exchange_gather(x, name, d):
+    devices = lax.axis_size(name)
+    parts = jnp.stack([x for _ in range(devices)])
+    parts = lax.all_to_all(parts, name, split_axis=0, concat_axis=0)
+    return jnp.concatenate(parts, axis=d)
 
 
 def rms_scale(values, gain):
@@ -52,7 +59,7 @@
     req = lax.axis_index(("y", "z"))
     ix, ic = (lax.axis_index("x"), lax.axis_index("c"))
     qkv_block = lax.all_gather(w_qkv[0, :, 0], "y", axis=0, tiled=True)
-    out_part = lax.all_gather(w_out[0].T, "z", axis=0, tiled=True)
+    out_part = exchange_gather(w_out[0].T, "z", 0)
     out_block = lax.all_gather(out_part, "y", axis=0, tiled=True)
     gate_up = jnp.concatenate([w_gate[0].T, w_up[0].T], axis=0)
     gate_up = lax.all_gather(gate_up, "x", axis=0)

time: 242 us -> 264 us (1.091)
  waiting for transfers between devices: 50.5 us -> 90.9 us
  blocking collectives: 96.2 us -> 69.6 us
  starting transfers between devices: 58.9 us -> 65.4 us
    all_gather x1, waiting for transfers between devices: 2.8 us -> 30.9 us  [local(): out_block = lax.all_gather(out_part, 'y', axis=0, tiled=True)]
    all_gather x1 -> x0, blocking collectives: 27 us -> none  [local(): out_part = lax.all_gather(w_out[0].T, 'z', axis=0, tiled=True)]
    all_to_all x0 -> x1, waiting for transfers between devices: none -> 12.3 us  [exchange_gather(): parts = lax.all_to_all(parts, name, split_axis=0, concat_axis=0)]
    all_to_all x0 -> x1, starting transfers between devices: none -> 3.53 us  [exchange_gather(): parts = lax.all_to_all(parts, name, split_axis=0, concat_axis=0)]
    all_to_all x5, starting transfers between devices: 58.8 us -> 61.8 us  [swap(): return lax.all_to_all(values, axes, split_axis=0, concat_axis=0, tiled=True)]
  transfers between devices with their start and end apart: 7 -> 8, of which waited for: 5 -> 6; matrix products, arithmetic and copies ran while one was open for 2% -> 1% of each run, Pallas kernels for 0% -> 0%
where the time goes in v1:
time: 264 us; the launch traced here: 263 us
  waiting for transfers between devices  90.9 us (34%)
  blocking collectives  69.6 us (26%)
  starting transfers between devices  65.4 us (25%)
  between operations  13.8 us (5%)
  other arithmetic  10.3 us (4%)
  local copies, waits for them, and re-layouts  9.21 us (3%)
  matrix products  3.4 us (1%)
    all_to_all x5, starting transfers between devices, swap(): return lax.all_to_all(values, axes, split_axis=0, concat_axis=0, tiled=True)  61.8 us
    all_to_all x5, waiting for transfers between devices, swap(): return lax.all_to_all(values, axes, split_axis=0, concat_axis=0, tiled=True)  32.3 us
    all_to_all x2, blocking collectives, swap(): return lax.all_to_all(values, axes, split_axis=0, concat_axis=0, tiled=True)  31.3 us
    all_gather x1, waiting for transfers between devices, local(): out_block = lax.all_gather(out_part, 'y', axis=0, tiled=True)  30.9 us
    all_gather x1, waiting for transfers between devices, local(): whole = lax.all_gather(piece, 'c', axis=0)  15.4 us
    all_to_all x1, waiting for transfers between devices, exchange_gather(): parts = lax.all_to_all(parts, name, split_axis=0, concat_axis=0)  12.3 us
    all_gather x1, blocking collectives, local(): qkv_block = lax.all_gather(w_qkv[0, :, 0], 'y', axis=0, tiled=True)  10.7 us
    all_gather x1, blocking collectives, local(): gate_up = lax.all_gather(gate_up, 'x', axis=0)  9.93 us
  transfers between devices with their start and end apart: 8, of which 6 were waited for; matrix products, arithmetic and copies ran while one was open for 1% of the time, Pallas kernels for 0%

profile of v1, /device:TPU:1, one launch (start us, length us, event | category | flops | bytes accessed | tf_op | source)
XLA Modules:
  0.0 262.7 jit_solution(6641081564966816011)
XLA Ops:
  6.5 0.9 fusion.26
  7.4 0.8 fusion.28
  9.1 15.7 %all-to-all-start = ((bf16[16,4,128]{2,1,0:T(4,128)(2,1)}), bf16[16,4,128]{2,1,0:T(4,128)(2,1)S(1)}, u32[]{:S(2)}, u32[]{:S(2)}) async-start(bf16[16,4,128]{2,1,0:T(4,128)(2,1)} %copy.39), calls=%async_computation | async-start | bytes 32768 | tf_op jit(solution)/shard_map/all_to_all | solution.py:32
  26.7 10.7 %all-gather = bf16[1,128,1,512]{3,1,2,0:T(8,128)(2,1)S(1)} all-gather(bf16[1,32,1,512]{3,1,2,0:T(8,128)(2,1)} %param.18), channel_id=2, replica_groups=mesh['y'=4,'z'=16,'x'=4,'c'=2] {'y'}, dimensions={1}, use_global_device_ids=true | all-gather | bytes 163840 | tf_op jit(solution)/shard_map/all_gather | solution.py:61
  38.2 10.6 %all-to-all-start.1 = ((bf16[16,4,512]{2,1,0:T(4,128)(2,1)}), bf16[16,4,512]{2,1,0:T(4,128)(2,1)S(1)}, u32[]{:S(2)}, u32[]{:S(2)}) async-start(bf16[16,4,512]{2,1,0:T(4,128)(2,1)} %reshape.267), calls=%async_computation.1 | async-start | bytes 131072 | tf_op jit(solution)/shard_map/all_to_all | solution.py:32
  48.9 11.4 %all-to-all-done.1 = bf16[16,4,512]{2,1,0:T(4,128)(2,1)S(1)} async-done(((bf16[16,4,512]{2,1,0:T(4,128)(2,1)}), bf16[16,4,512]{2,1,0:T(4,128)(2,1)S(1)}, u32[]{:S(2)}, u32[]{:S(2)}) %all-to-all-start.1) | async-done | bytes 65568 | tf_op jit(solution)/shard_map/all_to_all | solution.py:32
  61.1 3.5 %all-to-all-start.2 = ((bf16[16,32,256]{2,1,0:T(8,128)(2,1)}), bf16[16,32,256]{2,1,0:T(8,128)(2,1)S(1)}, u32[]{:S(2)}, u32[]{:S(2)}) async-start(bf16[16,32,256]{2,1,0:T(8,128)(2,1)} %stack.2), calls=%async_computation.2 | async-start | bytes 524288 | tf_op jit(solution)/shard_map/all_to_all | solution.py:16
  65.1 12.3 %all-to-all-done.2 = bf16[16,32,256]{2,1,0:T(8,128)(2,1)S(1)} async-done(((bf16[16,32,256]{2,1,0:T(8,128)(2,1)}), bf16[16,32,256]{2,1,0:T(8,128)(2,1)S(1)}, u32[]{:S(2)}, u32[]{:S(2)}) %all-to-all-start.2) | async-done | bytes 262176 | tf_op jit(solution)/shard_map/all_to_all | solution.py:16
  78.9 30.9 %all-gather.6.cloned.1.call-done = bf16[2048,256]{1,0:T(8,128)(2,1)} async-done(((bf16[512,256]{1,0:T(8,128)(2,1)}), bf16[2048,256]{1,0:T(8,128)(2,1)}) %all-gather.6.cloned.1.call-update) | async-done | bytes 1048592 | tf_op jit(solution)/shard_map/all_gather | solution.py:63
  109.8 1.7 fusion.14
  112.2 6.0 %all-to-all-start.3 = ((f32[8,4,2048]{2,1,0:T(4,128)}), f32[8,4,2048]{2,1,0:T(4,128)S(1)}, u32[]{:S(2)}, u32[]{:S(2)}) async-start(f32[8,4,2048]{2,1,0:T(4,128)} %broadcast_in_dim.26), calls=%async_computation.3 | async-start | bytes 524288 | tf_op jit(solution)/shard_map/all_to_all | solution.py:32
  118.2 6.5 %all-to-all-done.3 = f32[8,4,2048]{2,1,0:T(4,128)S(1)} async-done(((f32[8,4,2048]{2,1,0:T(4,128)}), f32[8,4,2048]{2,1,0:T(4,128)S(1)}, u32[]{:S(2)}, u32[]{:S(2)}) %all-to-all-start.3) | async-done | bytes 262176 | tf_op jit(solution)/shard_map/all_to_all | solution.py:32
  127.0 1.4 reduce.7
  129.2 14.4 %all-to-all-start.4 = ((bf16[64,2,512]{2,1,0:T(2,128)(2,1)}), bf16[64,2,512]{2,1,0:T(2,128)(2,1)S(1)}, u32[]{:S(2)}, u32[]{:S(2)}) async-start(bf16[64,2,512]{2,1,0:T(2,128)(2,1)} %reshape.290), calls=%async_computation.4 | async-start | bytes 262144 | tf_op jit(solution)/shard_map/all_to_all | solution.py:32
  143.6 9.8 %all_gather.30 = bf16[4,96,256]{2,1,0:T(8,128)(2,1)S(1)} all-gather(bf16[1,96,256]{2,1,0:T(8,128)(2,1)S(1)} %copy-done.7), channel_id=1, replica_groups=mesh['y'=4,'z'=16,'x'=4,'c'=2] {'x'}, dimensions={0}, use_global_device_ids=true | all-gather | bytes 245760 | tf_op jit(solution)/shard_map/all_gather | solution.py:66
  153.5 9.9 %all-gather.1 = bf16[768,256]{1,0:T(8,128)(2,1)S(1)} all-gather(bf16[192,256]{1,0:T(8,128)(2,1)S(1)} %pad_maximum_fusion), channel_id=3, replica_groups=mesh['y'=4,'z'=16,'x'=4,'c'=2] {'x'}, dimensions={0}, use_global_device_ids=true | all-gather | bytes 491520 | tf_op jit(solution)/shard_map/all_gather | solution.py:65
  164.2 7.9 %all-gather.2 = f32[128,192]{1,0:T(8,128)S(1)} all-gather(f32[64,192]{1,0:T(8,128)S(1)} %fusion.22), channel_id=4, replica_groups=mesh['y'=4,'z'=16,'x'=4,'c'=2] {'c'}, dimensions={0}, use_global_device_ids=true | all-gather | bytes 147456 | tf_op jit(solution)/shard_map/all_gather | solution.py:111
  173.8 15.1 %all-to-all-start.5 = ((bf16[64,2,512]{2,1,0:T(2,128)(2,1)}), bf16[64,2,512]{2,1,0:T(2,128)(2,1)S(1)}, u32[]{:S(2)}, u32[]{:S(2)}) async-start(bf16[64,2,512]{2,1,0:T(2,128)(2,1)} %reshape.292), calls=%async_computation.5 | async-start | bytes 262144 | tf_op jit(solution)/shard_map/all_to_all | solution.py:32
  189.0 14.4 %all-to-all-done.5 = bf16[64,2,512]{2,1,0:T(2,128)(2,1)S(1)} async-done(((bf16[64,2,512]{2,1,0:T(2,128)(2,1)}), bf16[64,2,512]{2,1,0:T(2,128)(2,1)S(1)}, u32[]{:S(2)}, u32[]{:S(2)}) %all-to-all-start.5) | async-done | bytes 131104 | tf_op jit(solution)/shard_map/all_to_all | solution.py:32
  203.9 1.4 reduce.9
  205.4 21.1 %all_to_all.40 = bf16[64,2,512]{2,1,0:T(2,128)(2,1)S(1)} all-to-all(bf16[64,2,512]{2,1,0:T(2,128)(2,1)S(1)} %reshape.294), channel_id=1, replica_groups=mesh['y'=4,'z'=16,'x'=4,'c'=2] {'y','z'}, dimensions={0} | all-to-all | bytes 262144 | tf_op jit(solution)/shard_map/all_to_all | solution.py:32
  226.8 10.1 %all_to_all.41 = bf16[4,64,1024]{2,1,0:T(8,128)(2,1)} all-to-all(bf16[4,64,1024]{2,1,0:T(8,128)(2,1)S(1)} %broadcast_in_dim.31), channel_id=1, replica_groups=mesh['y'=4,'z'=16,'x'=4,'c'=2] {'x'}, dimensions={0} | all-to-all | bytes 1048576 | tf_op jit(solution)/shard_map/all_to_all | solution.py:32
  237.1 15.4 %all-gather.8.cloned.1.call-done = bf16[2,256,1024]{2,1,0:T(8,128)(2,1)} async-done(((bf16[1,256,1024]{2,1,0:T(8,128)(2,1)}), bf16[2,256,1024]{2,1,0:T(8,128)(2,1)}) %all-gather.8.cloned.1.call-update) | async-done | bytes 1048592 | tf_op jit(solution)/shard_map/all_gather | solution.py:120
  252.5 1.6 fusion
  (103 shorter events, 15.1 us)
Async XLA Ops:
  6.5 42.2 %copy-start = (bf16[1,2048,2]{1,2,0:T(2,128)(2,1)S(1)}, bf16[1,2048,2]{1,2,0:T(2,128)(2,1)}, u32[]{:S(2)}) copy-start(bf16[1,2048,2]{1,2,0:T(2,128)(2,1)} %param.19) | copy-start | bytes 24580
  6.5 53.8 %copy-start.8 = (bf16[1,256,32]{1,2,0:T(8,128)(2,1)S(1)}, bf16[1,256,32]{1,2,0:T(8,128)(2,1)}, u32[]{:S(2)}) copy-start(bf16[1,256,32]{1,2,0:T(8,128)(2,1)} %param.20) | copy-start | bytes 49156
  6.5 58.4 %copy-start.11 = (f32[1,128]{1,0:T(1,128)S(1)}, f32[1,128]{1,0:T(1,128)}, u32[]{:S(2)}) copy-start(f32[1,128]{1,0:T(1,128)} %param.23) | copy-start | bytes 1540
  8.4 69.8 %copy-start.12 = (f32[1,128]{1,0:T(1,128)S(1)}, f32[1,128]{1,0:T(1,128)}, u32[]{:S(2)}) copy-start(f32[1,128]{1,0:T(1,128)} %param.22) | copy-start | bytes 1540
  8.4 70.1 %copy-start.13 = (bf16[1,2,1024,1,128]{4,2,3,1,0:T(8,128)(2,1)S(1)}, bf16[1,2,1024,1,128]{4,2,3,1,0:T(8,128)(2,1)}, u32[]{:S(2)}) copy-start(bf16[1,2,1024,1,128]{4,2,3,1,0:T(8,128)(2,1)} %param.17) | copy-start | bytes 1572868
  9.1 28.2 %all-to-all-start = ((bf16[16,4,128]{2,1,0:T(4,128)(2,1)}), bf16[16,4,128]{2,1,0:T(4,128)(2,1)S(1)}, u32[]{:S(2)}, u32[]{:S(2)}) async-start(bf16[16,4,128]{2,1,0:T(4,128)(2,1)} %copy.39), calls=%async_computation | async-start | bytes 32768 | tf_op jit(solution)/shard_map/all_to_all | solution.py:32
  38.2 22.2 %all-to-all-start.1 = ((bf16[16,4,512]{2,1,0:T(4,128)(2,1)}), bf16[16,4,512]{2,1,0:T(4,128)(2,1)S(1)}, u32[]{:S(2)}, u32[]{:S(2)}) async-start(bf16[16,4,512]{2,1,0:T(4,128)(2,1)} %reshape.267), calls=%async_computation.1 | async-start | bytes 131072 | tf_op jit(solution)/shard_map/all_to_all | solution.py:32
  61.1 16.3 %all-to-all-start.2 = ((bf16[16,32,256]{2,1,0:T(8,128)(2,1)}), bf16[16,32,256]{2,1,0:T(8,128)(2,1)S(1)}, u32[]{:S(2)}, u32[]{:S(2)}) async-start(bf16[16,32,256]{2,1,0:T(8,128)(2,1)} %stack.2), calls=%async_computation.2 | async-start | bytes 524288 | tf_op jit(solution)/shard_map/all_to_all | solution.py:16
  64.6 45.2 %all-gather.6.cloned.1.call-start = ((), (), s32[]{:S(2)}) async-start(), calls=%async_computation.8 | async-start | bytes 1310720 | tf_op jit(solution)/shard_map/all_gather | solution.py:63
  77.4 0.7 copy-start.3
  109.8 15.0 %copy-start.4 = (bf16[4,2048]{1,0:T(4,128)(2,1)S(1)}, bf16[4,2048]{1,0:T(4,128)(2,1)}, u32[]{:S(2)}) copy-start(bf16[4,2048]{1,0:T(4,128)(2,1)} %param.15) | copy-start | bytes 49156
  109.8 15.7 %copy-start.10 = (f32[1,2048]{1,0:T(1,128)S(1)}, f32[1,2048]{1,0:T(1,128)}, u32[]{:S(2)}) copy-start(f32[1,2048]{1,0:T(1,128)} %param.24) | copy-start | bytes 24580
  112.2 31.4 %copy-start.7 = (bf16[1,96,256]{2,1,0:T(8,128)(2,1)S(1)}, bf16[1,96,256]{2,1,0:T(8,128)(2,1)}, u32[]{:S(2)}) copy-start(bf16[1,96,256]{2,1,0:T(8,128)(2,1)} %param.27) | copy-start | bytes 147460
  112.2 12.5 %all-to-all-start.3 = ((f32[8,4,2048]{2,1,0:T(4,128)}), f32[8,4,2048]{2,1,0:T(4,128)S(1)}, u32[]{:S(2)}, u32[]{:S(2)}) async-start(f32[8,4,2048]{2,1,0:T(4,128)} %broadcast_in_dim.26), calls=%async_computation.3 | async-start | bytes 524288 | tf_op jit(solution)/shard_map/all_to_all | solution.py:32
  124.8 28.7 %copy-start.5 = (bf16[1,256,96]{1,2,0:T(8,128)(2,1)S(1)}, bf16[1,256,96]{1,2,0:T(8,128)(2,1)}, u32[]{:S(2)}) copy-start(bf16[1,256,96]{1,2,0:T(8,128)(2,1)} %param.26) | copy-start | bytes 147460
  124.8 28.7 %copy-start.6 = (bf16[1,256,96]{1,2,0:T(8,128)(2,1)S(1)}, bf16[1,256,96]{1,2,0:T(8,128)(2,1)}, u32[]{:S(2)}) copy-start(bf16[1,256,96]{1,2,0:T(8,128)(2,1)} %param.25) | copy-start | bytes 147460
  129.2 34.6 %all-to-all-start.4 = ((bf16[64,2,512]{2,1,0:T(2,128)(2,1)}), bf16[64,2,512]{2,1,0:T(2,128)(2,1)S(1)}, u32[]{:S(2)}, u32[]{:S(2)}) async-start(bf16[64,2,512]{2,1,0:T(2,128)(2,1)} %reshape.290), calls=%async_computation.4 | async-start | bytes 262144 | tf_op jit(solution)/shard_map/all_to_all | solution.py:32
  173.8 29.6 %all-to-all-start.5 = ((bf16[64,2,512]{2,1,0:T(2,128)(2,1)}), bf16[64,2,512]{2,1,0:T(2,128)(2,1)S(1)}, u32[]{:S(2)}, u32[]{:S(2)}) async-start(bf16[64,2,512]{2,1,0:T(2,128)(2,1)} %reshape.292), calls=%async_computation.5 | async-start | bytes 262144 | tf_op jit(solution)/shard_map/all_to_all | solution.py:32
  188.9 63.6 %all-gather.8.cloned.1.call-start = ((), (), s32[]{:S(2)}) async-start(), calls=%async_computation.9 | async-start | bytes 1572864 | tf_op jit(solution)/shard_map/all_gather | solution.py:120
  226.7 10.3 %copy-start.9 = (f32[2048]{0:T(1024)S(1)}, f32[2048]{0:T(1024)}, u32[]{:S(2)}) copy-start(f32[2048]{0:T(1024)} %param.28) | copy-start | bytes 24580
  226.7 10.3 %copy-start.2 = (bf16[2048,256]{1,0:T(8,128)(2,1)S(1)}, bf16[2048,256]{1,0:T(8,128)(2,1)}, u32[]{:S(2)}) copy-start(bf16[2048,256]{1,0:T(8,128)(2,1)} %param.29) | copy-start | bytes 3145732
  252.5 1.6 copy-start.1
Sparse Core Ops, SparseCore 0:
  78.2 31.4 all-gather.5
  237.1 15.3 all-gather.7
